TPU v7x, 32 devices: a whole 2x2x4 slice. The times are simulated.
32 devices in a mesh: wide: 8 (over z, y), narrow: 4 (over x, core).
Axes of the slice: x: 2, y: 2, z: 4, core: 2. Of those that a mesh axis runs over, the one named last changes fastest.
Arguments:
- image_tokens: bfloat16 [16, 1024, 1024], P('wide', 'narrow'), may hold values from -6 to 6
- text_states: bfloat16 [16, 128, 1024], P('wide', 'narrow'), may hold values from -6 to 6
- caption_lengths: int32 [16], P('wide'), may hold values from 1 to 128, as said below
- text_mask: int32 [16, 128], P('wide'), may hold values 0 or 1
- self_qkv: bfloat16 [3, 1024, 1024], replicated, may hold values from -0.1875 to 0.1875
- self_out: bfloat16 [1024, 1024], replicated, may hold values from -0.75 to 0.75
- cross_query: bfloat16 [1024, 1024], replicated, may hold values from -0.1875 to 0.1875
- cross_kv: bfloat16 [2, 1024, 1024], replicated, may hold values from -0.1875 to 0.1875
- cross_out: bfloat16 [1024, 1024], replicated, may hold values from -0.5 to 0.5
- mlp_in: bfloat16 [1024, 4096], replicated, may hold values from -0.1875 to 0.1875
- mlp_out: bfloat16 [4096, 1024], replicated, may hold values from -0.09375 to 0.09375
- norm_gains: float32 [3, 1024], replicated, may hold values from 0.1 to 1.9
- norm_shifts: float32 [3, 1024], replicated, may hold values from -3 to 3
- out_biases: float32 [3, 1024], replicated, may hold values from -3 to 3
- mlp_bias: float32 [4096], replicated, may hold values from -3 to 3
- cotangent: bfloat16 [16, 1024, 1024], P('wide', 'narrow'), may hold values from -6 to 6
Outputs:
- layer_out: float32 [16, 1024, 1024], P('wide', 'narrow')
- grad_image: float32 [16, 1024, 1024], P('wide', 'narrow')
- grad_text: float32 [16, 128, 1024], P('wide', 'narrow')
- grad_self_qkv: float32 [3, 1024, 1024], P(None, 'wide', 'narrow')
- grad_self_out: float32 [1024, 1024], P('wide', 'narrow')
- grad_cross_query: float32 [1024, 1024], P('wide', 'narrow')
- grad_cross_kv: float32 [2, 1024, 1024], P(None, 'wide', 'narrow')
- grad_cross_out: float32 [1024, 1024], P('wide', 'narrow')
- grad_mlp_in: float32 [1024, 4096], P('wide', 'narrow')
- grad_mlp_out: float32 [4096, 1024], P('wide', 'narrow')
- grad_norm_gains: float32 [3, 1024], replicated
- grad_norm_shifts: float32 [3, 1024], replicated
- grad_out_biases: float32 [3, 1024], replicated
- grad_mlp_bias: float32 [4096], replicated
Inputs may be any that keep to these rules, and one draw needn't show every extreme that they name: `caption_lengths`: in every aligned block of 2 items, one caption has all 128 slots.
All inputs are finite; a program needn't handle non-finite values. No bound on the sum of `text_mask` on one device may be relied on, other than what follows from the above.
Results may differ from a plain program's by a relative error of at most 0.023.
Values may be sent and summed in bfloat16 or wider, within the bound.
No kernel may reach another device: no remote copies, remote signals or barrier semaphores. Data moves between devices by JAX's collectives and lax.ppermute only.
A program may use at most 384 MiB of HBM per device.

v0:
```python
from functools import partial

import jax
import jax.numpy as jnp
from jax import lax
from jax.sharding import PartitionSpec as P

HEADS = 16
HEAD_DIM = 64


def gelu_tanh(pre_act):
    return (
        0.5
        * pre_act
        * (1.0 + jnp.tanh(0.7978845608028654 * (pre_act + 0.044715 * pre_act * pre_act * pre_act)))
    )


def layer_norm(hidden, gain, shift):
    centered = hidden - jnp.mean(hidden, -1, keepdims=True)
    inverse = lax.rsqrt(jnp.mean(centered * centered, -1, keepdims=True) + 1e-05)
    unit_rows = centered * inverse
    return (unit_rows * gain + shift, unit_rows, inverse)


def norm_back(grad_out, gain, unit_rows, inverse):
    grad_unit = grad_out * gain
    grad_in = inverse * (
        grad_unit
        - jnp.mean(grad_unit, -1, keepdims=True)
        - unit_rows * jnp.mean(grad_unit * unit_rows, -1, keepdims=True)
    )
    return (grad_in, jnp.sum(grad_out * unit_rows, 0), jnp.sum(grad_out, 0))


def masked_scores(queries, keys_all, allowed, score_scale):
    raw_scores = (
        jnp.einsum("bqhd,bkhd->bhqk", queries, keys_all, preferred_element_type=jnp.float32)
        * score_scale
    )
    return jnp.where(allowed[:, None], raw_scores, -1e30)


def attend_block(queries, keys_all, values_all, allowed, score_scale):
    scores = masked_scores(queries, keys_all, allowed, score_scale)
    top_score = jnp.max(scores, -1, keepdims=True)
    expo = jnp.exp(scores - top_score)
    total = jnp.sum(expo, -1, keepdims=True)
    weights = (expo / total).astype(jnp.bfloat16)
    output = jnp.einsum("bhqk,bkhd->bqhd", weights, values_all, preferred_element_type=jnp.float32)
    return (output, top_score + jnp.log(total))


def attend_back(queries, keys_all, values_all, allowed, grad_out, log_total, score_scale):
    scores = masked_scores(queries, keys_all, allowed, score_scale)
    probs = jnp.exp(scores - log_total)
    grad_probs = jnp.einsum(
        "bqhd,bkhd->bhqk", grad_out, values_all, preferred_element_type=jnp.float32
    )
    inner = jnp.sum(probs * grad_probs, -1, keepdims=True)
    grad_scores = (probs * (grad_probs - inner)).astype(jnp.bfloat16)
    grad_query = (
        jnp.einsum("bhqk,bkhd->bqhd", grad_scores, keys_all, preferred_element_type=jnp.float32)
        * score_scale
    )
    grad_keys = (
        jnp.einsum("bhqk,bqhd->bkhd", grad_scores, queries, preferred_element_type=jnp.float32)
        * score_scale
    )
    grad_values = jnp.einsum(
        "bhqk,bqhd->bkhd", probs.astype(jnp.bfloat16), grad_out, preferred_element_type=jnp.float32
    )
    return (grad_query, grad_keys, grad_values)


def pick_group(item_count, query_len):
    group_size = 1
    while (
        group_size * 2 <= item_count
        and item_count % (group_size * 2) == 0
        and (group_size * query_len < 512)
    ):
        group_size = group_size * 2
    return group_size


def by_groups(function, arrays, group_size):

    def regroup(member):
        return member.reshape((member.shape[0] // group_size, group_size) + member.shape[1:])

    def flatten(member):
        return member.reshape((member.shape[0] * member.shape[1],) + member.shape[2:])

    def apply_group(grouped):
        return function(*grouped)

    results = lax.map(apply_group, tuple((regroup(member) for member in arrays)))
    return tuple((flatten(member) for member in results))


def body(
    image_tokens,
    text_states,
    caption_lengths,
    text_mask,
    self_qkv,
    self_out,
    cross_query,
    cross_kv,
    cross_out,
    mlp_in,
    mlp_out,
    norm_gains,
    norm_shifts,
    out_biases,
    mlp_bias,
    cotangent,
):
    item_count, local_len, model_width = image_tokens.shape
    row_count = item_count * local_len
    full_len = local_len * lax.axis_size("narrow")
    text_local = text_states.shape[1]
    text_full = text_mask.shape[1]
    score_scale = HEAD_DIM ** (-0.5)
    group_size = pick_group(item_count, local_len)
    forward_fn = partial(attend_block, score_scale=score_scale)
    backward_fn = partial(attend_back, score_scale=score_scale)
    slot_index = jnp.arange(text_full)
    live_slots = (slot_index[None, :] < caption_lengths[:, None]) & (
        (text_mask == 1) | (slot_index[None, :] == 0)
    )
    text_allowed = jnp.broadcast_to(live_slots[:, None, :], (item_count, local_len, text_full))

    def split_heads(matrix, length):
        return matrix.reshape(item_count, length, HEADS, HEAD_DIM)

    residual_in = image_tokens.reshape(row_count, model_width).astype(jnp.float32)
    normed_one, unit_one, inverse_one = layer_norm(residual_in, norm_gains[0], norm_shifts[0])
    input_one = normed_one.astype(jnp.bfloat16)
    projected = jnp.einsum(
        "rd,jde->jre", input_one, self_qkv, preferred_element_type=jnp.float32
    ).astype(jnp.bfloat16)
    position = lax.axis_index("narrow") * local_len + jnp.arange(local_len)
    causal = jnp.arange(full_len)[None, :] <= position[:, None]
    self_allowed = jnp.broadcast_to(causal[None], (item_count, local_len, full_len))
    queries_self = split_heads(projected[0], local_len)
    keys_local = projected[1].reshape(item_count, local_len, model_width)
    values_local = projected[2].reshape(item_count, local_len, model_width)
    keys_self, values_self = (
        lax.all_gather(keys_local, "narrow", axis=1, tiled=True),
        lax.all_gather(values_local, "narrow", axis=1, tiled=True),
    )
    keys_self = split_heads(keys_self, full_len)
    values_self = split_heads(values_self, full_len)
    attn_self, logsum_self = by_groups(
        forward_fn, (queries_self, keys_self, values_self, self_allowed), group_size
    )
    mixed_self = attn_self.reshape(row_count, model_width).astype(jnp.bfloat16)
    after_self = (
        residual_in
        + jnp.dot(mixed_self, self_out, preferred_element_type=jnp.float32)
        + out_biases[0]
    )
    normed_two, unit_two, inverse_two = layer_norm(after_self, norm_gains[1], norm_shifts[1])
    input_two = normed_two.astype(jnp.bfloat16)
    queries_cross = split_heads(
        jnp.dot(input_two, cross_query, preferred_element_type=jnp.float32).astype(jnp.bfloat16),
        local_len,
    )
    text_flat = text_states.reshape(item_count * text_local, model_width)
    text_proj = jnp.einsum(
        "rd,jde->jre", text_flat, cross_kv, preferred_element_type=jnp.float32
    ).astype(jnp.bfloat16)
    text_keys_local = text_proj[0].reshape(item_count, text_local, model_width)
    text_values_local = text_proj[1].reshape(item_count, text_local, model_width)
    text_keys, text_values = (
        lax.all_gather(text_keys_local, "narrow", axis=1, tiled=True),
        lax.all_gather(text_values_local, "narrow", axis=1, tiled=True),
    )
    text_keys = split_heads(text_keys, text_full)
    text_values = split_heads(text_values, text_full)
    attn_cross, logsum_cross = by_groups(
        forward_fn, (queries_cross, text_keys, text_values, text_allowed), group_size
    )
    mixed_cross = attn_cross.reshape(row_count, model_width).astype(jnp.bfloat16)
    after_cross = (
        after_self
        + jnp.dot(mixed_cross, cross_out, preferred_element_type=jnp.float32)
        + out_biases[1]
    )
    normed_three, unit_three, inverse_three = layer_norm(after_cross, norm_gains[2], norm_shifts[2])
    input_three = normed_three.astype(jnp.bfloat16)
    pre_act = jnp.dot(input_three, mlp_in, preferred_element_type=jnp.float32) + mlp_bias
    activated, gelu_pull = jax.vjp(gelu_tanh, pre_act)
    hidden_act = activated.astype(jnp.bfloat16)
    layer_out = (
        after_cross
        + jnp.dot(hidden_act, mlp_out, preferred_element_type=jnp.float32)
        + out_biases[2]
    )
    grad_out = cotangent.reshape(row_count, model_width).astype(jnp.float32)
    branch_three = grad_out.astype(jnp.bfloat16)
    bias_three = jnp.sum(branch_three.astype(jnp.float32), 0)
    weight_down = jnp.einsum(
        "rf,rd->fd", hidden_act, branch_three, preferred_element_type=jnp.float32
    )
    grad_hidden = jnp.einsum(
        "rd,fd->rf", branch_three, mlp_out, preferred_element_type=jnp.float32
    ).astype(jnp.bfloat16)
    (grad_pre,) = gelu_pull(grad_hidden.astype(jnp.float32))
    grad_pre_low = grad_pre.astype(jnp.bfloat16)
    bias_hidden = jnp.sum(grad_pre_low.astype(jnp.float32), 0)
    weight_up = jnp.einsum(
        "rd,rf->df", input_three, grad_pre_low, preferred_element_type=jnp.float32
    )
    grad_normed_three = jnp.einsum(
        "rf,df->rd", grad_pre_low, mlp_in, preferred_element_type=jnp.float32
    )
    grad_in_three, gain_three, shift_three = norm_back(
        grad_normed_three, norm_gains[2], unit_three, inverse_three
    )
    grad_cross_res = grad_out + grad_in_three
    branch_two = grad_cross_res.astype(jnp.bfloat16)
    bias_two = jnp.sum(branch_two.astype(jnp.float32), 0)
    weight_cross_out = jnp.einsum(
        "rd,re->de", mixed_cross, branch_two, preferred_element_type=jnp.float32
    )
    grad_mixed_cross = jnp.einsum(
        "re,de->rd", branch_two, cross_out, preferred_element_type=jnp.float32
    ).astype(jnp.bfloat16)
    grad_cross_q, grad_text_k, grad_text_v = by_groups(
        backward_fn,
        (
            queries_cross,
            text_keys,
            text_values,
            text_allowed,
            split_heads(grad_mixed_cross, local_len),
            logsum_cross,
        ),
        group_size,
    )
    grad_cross_low = grad_cross_q.reshape(row_count, model_width).astype(jnp.bfloat16)
    weight_cross_query = jnp.einsum(
        "rd,re->de", input_two, grad_cross_low, preferred_element_type=jnp.float32
    )
    grad_normed_two = jnp.einsum(
        "re,de->rd", grad_cross_low, cross_query, preferred_element_type=jnp.float32
    )
    text_key_sum, text_value_sum = (
        lax.psum_scatter(
            grad_text_k.reshape(item_count, text_full, model_width).astype(jnp.bfloat16),
            "narrow",
            scatter_dimension=1,
            tiled=True,
        ).astype(jnp.float32),
        lax.psum_scatter(
            grad_text_v.reshape(item_count, text_full, model_width).astype(jnp.bfloat16),
            "narrow",
            scatter_dimension=1,
            tiled=True,
        ).astype(jnp.float32),
    )
    text_grads_low = jnp.stack(
        [
            text_key_sum.reshape(item_count * text_local, model_width),
            text_value_sum.reshape(item_count * text_local, model_width),
        ]
    ).astype(jnp.bfloat16)
    weight_cross_kv = jnp.einsum(
        "rd,jre->jde", text_flat, text_grads_low, preferred_element_type=jnp.float32
    )
    grad_text = jnp.einsum(
        "jre,jde->rd", text_grads_low, cross_kv, preferred_element_type=jnp.float32
    )
    grad_text = grad_text.reshape(item_count, text_local, model_width)
    grad_in_two, gain_two, shift_two = norm_back(
        grad_normed_two, norm_gains[1], unit_two, inverse_two
    )
    grad_self_res = grad_cross_res + grad_in_two
    branch_one = grad_self_res.astype(jnp.bfloat16)
    bias_one = jnp.sum(branch_one.astype(jnp.float32), 0)
    weight_self_out = jnp.einsum(
        "rd,re->de", mixed_self, branch_one, preferred_element_type=jnp.float32
    )
    grad_mixed_self = jnp.einsum(
        "re,de->rd", branch_one, self_out, preferred_element_type=jnp.float32
    ).astype(jnp.bfloat16)
    grad_query_self, grad_keys_self, grad_values_self = by_groups(
        backward_fn,
        (
            queries_self,
            keys_self,
            values_self,
            self_allowed,
            split_heads(grad_mixed_self, local_len),
            logsum_self,
        ),
        group_size,
    )
    key_grad_sum, value_grad_sum = (
        lax.psum_scatter(
            grad_keys_self.reshape(item_count, full_len, model_width).astype(jnp.bfloat16),
            "narrow",
            scatter_dimension=1,
            tiled=True,
        ).astype(jnp.float32),
        lax.psum_scatter(
            grad_values_self.reshape(item_count, full_len, model_width).astype(jnp.bfloat16),
            "narrow",
            scatter_dimension=1,
            tiled=True,
        ).astype(jnp.float32),
    )
    self_grads_low = jnp.stack(
        [
            grad_query_self.reshape(row_count, model_width),
            key_grad_sum.reshape(row_count, model_width),
            value_grad_sum.reshape(row_count, model_width),
        ]
    ).astype(jnp.bfloat16)
    weight_qkv = jnp.einsum(
        "rd,jre->jde", input_one, self_grads_low, preferred_element_type=jnp.float32
    )
    grad_normed_one = jnp.einsum(
        "jre,jde->rd", self_grads_low, self_qkv, preferred_element_type=jnp.float32
    )
    grad_in_one, gain_one, shift_one = norm_back(
        grad_normed_one, norm_gains[0], unit_one, inverse_one
    )
    grad_image = (grad_self_res + grad_in_one).reshape(item_count, local_len, model_width)
    part_qkv, part_sout, part_cq, part_ckv, part_cout, part_up, part_down = (
        lax.psum_scatter(
            weight_qkv.astype(jnp.bfloat16), "wide", scatter_dimension=1, tiled=True
        ).astype(jnp.float32),
        lax.psum_scatter(
            weight_self_out[None].astype(jnp.bfloat16), "wide", scatter_dimension=1, tiled=True
        ).astype(jnp.float32),
        lax.psum_scatter(
            weight_cross_query[None].astype(jnp.bfloat16), "wide", scatter_dimension=1, tiled=True
        ).astype(jnp.float32),
        lax.psum_scatter(
            weight_cross_kv.astype(jnp.bfloat16), "wide", scatter_dimension=1, tiled=True
        ).astype(jnp.float32),
        lax.psum_scatter(
            weight_cross_out[None].astype(jnp.bfloat16), "wide", scatter_dimension=1, tiled=True
        ).astype(jnp.float32),
        lax.psum_scatter(
            weight_up[None].astype(jnp.bfloat16), "wide", scatter_dimension=1, tiled=True
        ).astype(jnp.float32),
        lax.psum_scatter(
            weight_down[None].astype(jnp.bfloat16), "wide", scatter_dimension=1, tiled=True
        ).astype(jnp.float32),
    )
    sum_qkv, sum_sout, sum_cq, sum_ckv, sum_cout, sum_up, sum_down = (
        lax.psum_scatter(
            part_qkv.astype(jnp.bfloat16), "narrow", scatter_dimension=2, tiled=True
        ).astype(jnp.float32),
        lax.psum_scatter(
            part_sout.astype(jnp.bfloat16), "narrow", scatter_dimension=2, tiled=True
        ).astype(jnp.float32),
        lax.psum_scatter(
            part_cq.astype(jnp.bfloat16), "narrow", scatter_dimension=2, tiled=True
        ).astype(jnp.float32),
        lax.psum_scatter(
            part_ckv.astype(jnp.bfloat16), "narrow", scatter_dimension=2, tiled=True
        ).astype(jnp.float32),
        lax.psum_scatter(
            part_cout.astype(jnp.bfloat16), "narrow", scatter_dimension=2, tiled=True
        ).astype(jnp.float32),
        lax.psum_scatter(
            part_up.astype(jnp.bfloat16), "narrow", scatter_dimension=2, tiled=True
        ).astype(jnp.float32),
        lax.psum_scatter(
            part_down.astype(jnp.bfloat16), "narrow", scatter_dimension=2, tiled=True
        ).astype(jnp.float32),
    )
    gain_sum, shift_sum, bias_sum, hidden_bias_sum = lax.psum(
        (
            jnp.stack([gain_one, gain_two, gain_three]),
            jnp.stack([shift_one, shift_two, shift_three]),
            jnp.stack([bias_one, bias_two, bias_three]),
            bias_hidden,
        ),
        ("wide", "narrow"),
    )
    return (
        layer_out.reshape(item_count, local_len, model_width),
        grad_image,
        grad_text,
        sum_qkv,
        sum_sout[0],
        sum_cq[0],
        sum_ckv,
        sum_cout[0],
        sum_up[0],
        sum_down[0],
        gain_sum,
        shift_sum,
        bias_sum,
        hidden_bias_sum,
    )


def solution(mesh):
    placed = (
        P("wide", "narrow", None),
        P("wide", "narrow", None),
        P("wide"),
        P("wide", None),
        P(),
        P(),
        P(),
        P(),
        P(),
        P(),
        P(),
        P(),
        P(),
        P(),
        P(),
        P("wide", "narrow", None),
    )
    return jax.shard_map(
        body,
        mesh=mesh,
        in_specs=placed,
        out_specs=(
            P("wide", "narrow", None),
            P("wide", "narrow", None),
            P("wide", "narrow", None),
            P(None, "wide", "narrow"),
            P("wide", "narrow"),
            P("wide", "narrow"),
            P(None, "wide", "narrow"),
            P("wide", "narrow"),
            P("wide", "narrow"),
            P("wide", "narrow"),
            P(),
            P(),
            P(),
            P(),
        ),
        check_vma=False,
    )
```

profile of v0, /device:TPU:0, one launch (start us, length us, event | category | flops | bytes accessed | tf_op | source)
XLA Modules:
  0.0 1245.9 jit_solution(8111012778251985607)
XLA Ops:
  69.0 16.4 %fusion.69 = (f32[2,16,256]{2,1,0:T(8,128)S(1)}, f32[2,16,256,1024]{3,2,1,0:T(8,128)}) fusion(bf16[2,256,16,64]{1,3,2,0:T(8,128)(2,1)S(1)} %copy.88, bf16[2,1024,16,64]{1,3,2,0:T(8,128)(2,1)} %bitcast.218, pred[256,1024]{1,0:T(8,128)(4,1)S(1)} %iota_compare_fusion), kind=kOutput, calls=%fused_computation.156 | convolution fusion | flops 1098899456 | bytes 39092224 | tf_op jit(solution)/shard_map/while/body/eval_jaxpr/bqhd,bkhd->bhqk/dot_general | solution.py:39
  85.3 14.4 %fusion = f32[2,16,256]{2,1,0:T(8,128)S(1)} fusion(f32[2,16,256,1024]{3,2,1,0:T(8,128)} %get-tuple-element.197, f32[2,16,256]{2,1,0:T(8,128)S(1)} %get-tuple-element.196), kind=kLoop, calls=%fused_computation.6 | loop fusion | flops 16769024 | bytes 33619968 | tf_op jit(solution)/shard_map/while/body/eval_jaxpr/reduce_sum | solution.py:49
  106.0 15.2 %fusion.44 = bf16[2,256,16,64]{1,3,2,0:T(8,128)(2,1)S(1)} fusion(bf16[2,1024,16,64]{1,3,2,0:T(8,128)(2,1)} %bitcast.221, f32[2,16,256,1024]{3,2,1,0:T(8,128)} %get-tuple-element.197, f32[2,16,256]{2,1,0:T(8,128)S(1)} %fusion, f32[2,16,256]{2,1,0:T(8,128)S(1)} %get-tuple-element.196), kind=kOutput, calls=%fused_computation.103 | convolution fusion | flops 1099431936 | bytes 38862848 | tf_op jit(solution)/shard_map/while/body/eval_jaxpr/bhqk,bkhd->bqhd/dot_general | solution.py:51
  149.4 16.3 %convert_reduce_fusion = (f32[4096]{0:T(1024)}, bf16[512,4096]{1,0:T(8,128)(2,1)}) fusion(bf16[512,1024]{1,0:T(8,128)(2,1)S(1)} %bitcast.230, bf16[4096,1024]{1,0:T(8,128)(2,1)} %param.26, f32[512,4096]{1,0:T(8,128)} %fusion.63, f32[4096]{0:T(1024)S(1)} %copy-done.54), kind=kOutput, calls=%fused_computation.26 | convolution fusion | flops 4355780608 | bytes 22052864 | tf_op jit(solution)/shard_map/rd,fd->rf/dot_general | solution.py:209
  233.0 15.5 %fusion.17 = bf16[2,16,64,1024]{3,2,1,0:T(8,128)(2,1)} fusion(bf16[2,256,16,64]{1,3,2,0:T(8,128)(2,1)S(1)} %copy.101, f32[2,16,256,1024]{3,2,1,0:T(8,128)} %get-tuple-element.197, f32[2,16,256]{2,1,0:T(8,128)S(1)} %log_add_fusion), kind=kOutput, calls=%fused_computation.44 | convolution fusion | flops 1092616192 | bytes 38830080 | tf_op jit(solution)/shard_map/while/body/eval_jaxpr/bhqk,bqhd->bkhd/dot_general | solution.py:71
  248.9 24.0 %multiply_reduce_fusion = (f32[2,16,256]{2,1,0:T(8,128)S(1)}, f32[2,16,256,1024]{3,2,1,0:T(8,128)}) fusion(f32[2,16,256,1024]{3,2,1,0:T(8,128)} %get-tuple-element.197, f32[2,16,256]{2,1,0:T(8,128)S(1)} %log_add_fusion, bf16[2,256,16,64]{1,3,2,0:T(8,128)(2,1)S(1)} %copy.101, bf16[2,1024,16,64]{1,3,2,0:T(8,128)(2,1)} %bitcast.222), kind=kOutput, calls=%fused_computation.1 | convolution fusion | flops 1098899456 | bytes 72417280 | tf_op jit(solution)/shard_map/while/body/eval_jaxpr/bqhd,bkhd->bhqk/dot_general | solution.py:58
  272.9 28.2 %multiply_convert_fusion = bf16[2,16,256,1024]{3,2,1,0:T(8,128)(2,1)} fusion(f32[2,16,256,1024]{3,2,1,0:T(8,128)} %get-tuple-element.209, f32[2,16,256,1024]{3,2,1,0:T(8,128)} %get-tuple-element.197, f32[2,16,256]{2,1,0:T(8,128)S(1)} %get-tuple-element.208, f32[2,16,256]{2,1,0:T(8,128)S(1)} %log_add_fusion), kind=kLoop, calls=%fused_computation | loop fusion | flops 33554432 | bytes 83951616 | tf_op jit(solution)/shard_map/while/body/eval_jaxpr/convert_element_type | solution.py:62
  337.3 13.4 %convert_bitcast_fusion = bf16[1,4096,1024]{2,1,0:T(8,128)(2,1)} fusion(bf16[512,1024]{1,0:T(8,128)(2,1)S(1)} %bitcast.231, f32[512,4096]{1,0:T(8,128)} %fusion.63, f32[4096]{0:T(1024)S(1)} %copy-done.54), kind=kOutput, calls=%fused_computation.27 | convolution fusion | flops 4320133120 | bytes 17842176 | tf_op jit(solution)/shard_map/rf,rd->fd/dot_general | solution.py:206
  362.1 22.1 %reduce-scatter.31.cloned.1.call-done = bf16[1,128,1024]{2,1,0:T(8,128)(2,1)} async-done(((bf16[1,1024,1024]{2,1,0:T(8,128)(2,1)}), bf16[1,128,1024]{2,1,0:T(8,128)(2,1)}) %reduce-scatter.31.cloned.1.call-update) | async-done | bytes 262160 | tf_op jit(solution)/shard_map/reduce_scatter | solution.py:341
  384.4 13.2 %fusion.43 = bf16[2,256,16,64]{1,3,2,0:T(8,128)(2,1)} fusion(bf16[2,1024,16,64]{1,3,2,0:T(8,128)(2,1)} %bitcast.219, bf16[2,16,256,1024]{3,2,1,0:T(8,128)(2,1)} %multiply_convert_fusion), kind=kOutput, calls=%fused_computation.101 | convolution fusion | flops 1074790400 | bytes 22020096 | tf_op jit(solution)/shard_map/while/body/eval_jaxpr/bhqk,bkhd->bqhd/dot_general | solution.py:64
  405.5 49.1 %reduce-scatter.27.cloned.1.call-done = bf16[1,128,1024]{2,1,0:T(8,128)(2,1)} async-done(((bf16[1,1024,1024]{2,1,0:T(8,128)(2,1)}), bf16[1,128,1024]{2,1,0:T(8,128)(2,1)}) %reduce-scatter.27.cloned.1.call-update) | async-done | bytes 262160 | tf_op jit(solution)/shard_map/reduce_scatter | solution.py:338
  455.0 46.0 %reduce-scatter.23.cloned.1.call-done = bf16[2,256,1024]{1,2,0:T(8,128)(2,1)} async-done(((bf16[2,1024,1024]{1,2,0:T(8,128)(2,1)}), bf16[2,256,1024]{1,2,0:T(8,128)(2,1)}) %reduce-scatter.23.cloned.1.call-update) | async-done | bytes 1048592 | tf_op jit(solution)/shard_map/reduce_scatter | solution.py:310
  503.2 44.8 %reduce-scatter.21.cloned.1.call-done = bf16[2,256,1024]{1,2,0:T(8,128)(2,1)} async-done(((bf16[2,1024,1024]{1,2,0:T(8,128)(2,1)}), bf16[2,256,1024]{1,2,0:T(8,128)(2,1)}) %reduce-scatter.21.cloned.1.call-update) | async-done | bytes 1048592 | tf_op jit(solution)/shard_map/reduce_scatter | solution.py:304
  558.7 14.5 %copy.125 = bf16[3,1024,1024]{2,0,1:T(4,128)(2,1)} copy(bf16[3,1024,1024]{1,2,0:T(8,128)(2,1)} %convert_bitcast_fusion.2) | data formatting | bytes 12582912
  583.6 56.5 %reduce-scatter.51.cloned.1.call-done = bf16[128,2048]{1,0:T(8,128)(2,1)} async-done(((bf16[1024,2048]{1,0:T(8,128)(2,1)}), bf16[128,2048]{1,0:T(8,128)(2,1)}) %reduce-scatter.51.cloned.1.call-update) | async-done | bytes 524304
  644.6 147.8 %reduce-scatter.45.cloned.1.call-done = bf16[1,512,1024]{2,1,0:T(8,128)(2,1)} async-done(((bf16[1,4096,1024]{2,1,0:T(8,128)(2,1)}), bf16[1,512,1024]{2,1,0:T(8,128)(2,1)}) %reduce-scatter.45.cloned.1.call-update) | async-done | bytes 1048592 | tf_op jit(solution)/shard_map/reduce_scatter | solution.py:353
  805.2 139.3 %reduce-scatter.41.cloned.1.call-done = bf16[1,128,4096]{2,1,0:T(8,128)(2,1)} async-done(((bf16[1,1024,4096]{2,1,0:T(8,128)(2,1)}), bf16[1,128,4096]{2,1,0:T(8,128)(2,1)}) %reduce-scatter.41.cloned.1.call-update) | async-done | bytes 1048592 | tf_op jit(solution)/shard_map/reduce_scatter | solution.py:350
  949.0 16.8 %reduce-scatter.39.cloned.1.call-done = bf16[1,128,256]{2,1,0:T(8,128)(2,1)} async-done(((bf16[1,128,1024]{2,1,0:T(8,128)(2,1)}), bf16[1,128,256]{2,1,0:T(8,128)(2,1)}) %reduce-scatter.39.cloned.1.call-update) | async-done | bytes 65552 | tf_op jit(solution)/shard_map/reduce_scatter | solution.py:370
  967.3 21.2 %reduce-scatter.33.cloned.1.call-done = bf16[1,128,256]{2,1,0:T(8,128)(2,1)} async-done(((bf16[1,128,1024]{2,1,0:T(8,128)(2,1)}), bf16[1,128,256]{2,1,0:T(8,128)(2,1)}) %reduce-scatter.33.cloned.1.call-update) | async-done | bytes 65552 | tf_op jit(solution)/shard_map/reduce_scatter | solution.py:364
  990.0 20.9 %reduce-scatter.29.cloned.1.call-done = bf16[1,128,256]{2,1,0:T(8,128)(2,1)} async-done(((bf16[1,128,1024]{2,1,0:T(8,128)(2,1)}), bf16[1,128,256]{2,1,0:T(8,128)(2,1)}) %reduce-scatter.29.cloned.1.call-update) | async-done | bytes 65552 | tf_op jit(solution)/shard_map/reduce_scatter | solution.py:361
  1020.8 112.0 %reduce-scatter.49.cloned.1.call-done = bf16[128,3072]{1,0:T(8,128)(2,1)} async-done(((bf16[1024,3072]{1,0:T(8,128)(2,1)}), bf16[128,3072]{1,0:T(8,128)(2,1)}) %reduce-scatter.49.cloned.1.call-update) | async-done | bytes 786448
  1137.2 40.6 %all-reduce.2 = (f32[3,1024]{1,0:T(4,128)}, f32[3,1024]{1,0:T(4,128)}, f32[3,1024]{1,0:T(4,128)}, f32[4096]{0:T(1024)}) all-reduce(f32[3,1024]{1,0:T(4,128)S(1)} %pad_maximum_fusion.6, f32[3,1024]{1,0:T(4,128)S(1)} %pad_maximum_fusion.7, ...), channel_id=1, replica_groups=mesh['wide'=8,'narrow'=4] {'wide','narrow'}, use_global_device_ids=true, to_apply=%region_39.40 | all-reduce | flops 13312 | bytes 106496 | tf_op jit(solution)/shard_map/psum | solution.py:380
  1185.8 25.7 %reduce-scatter.43.cloned.1.call-done = bf16[1,128,1024]{2,1,0:T(8,128)(2,1)} async-done(((bf16[1,128,4096]{2,1,0:T(8,128)(2,1)}), bf16[1,128,1024]{2,1,0:T(8,128)(2,1)}) %reduce-scatter.43.cloned.1.call-update) | async-done | bytes 262160 | tf_op jit(solution)/shard_map/reduce_scatter | solution.py:373
  1213.2 24.0 %reduce-scatter.25.cloned.1.call-done = bf16[3,128,256]{1,2,0:T(8,128)(2,1)} async-done(((bf16[3,128,1024]{1,2,0:T(8,128)(2,1)}), bf16[3,128,256]{1,2,0:T(8,128)(2,1)}) %reduce-scatter.25.cloned.1.call-update) | async-done | bytes 196624 | tf_op jit(solution)/shard_map/reduce_scatter | solution.py:358
  (270 shorter events, 292.2 us)
Async XLA Ops:
  7.2 118.7 %copy-start = (bf16[1024,1024]{1,0:T(8,128)(2,1)S(1)}, bf16[1024,1024]{1,0:T(8,128)(2,1)}, u32[]{:S(2)}) copy-start(bf16[1024,1024]{1,0:T(8,128)(2,1)} %param.22) | copy-start | bytes 6291460
  7.2 55.5 %all-gather.5.cloned.1.call-start = ((), (), s32[]{:S(2)}) async-start(), calls=%async_computation.17 | async-start | bytes 5242880 | tf_op jit(solution)/shard_map/all_gather | solution.py:152
  12.2 129.7 %copy-start.48 = (f32[1,1024]{1,0:T(1,128)}, f32[1,1024]{1,0:T(1,128)S(1)}, u32[]{:S(2)}) copy-start(f32[1,1024]{1,0:T(1,128)S(1)} %get-tuple-element.188) | copy-start | bytes 12292
  22.6 77.2 %all-gather.3.cloned.1.call-start = ((), (), s32[]{:S(2)}) async-start(), calls=%async_computation.16 | async-start | bytes 5242880 | tf_op jit(solution)/shard_map/all_gather | solution.py:153
  23.3 290.5 %all-reduce.6.cloned.1.call-start = ((), (), s32[]{:S(2)}) async-start(), calls=%async_computation.34 | async-start | bytes 2097152
  205.2 156.4 %reduce-scatter.37.cloned.1.call-start = ((), (), s32[]{:S(2)}) async-start(), calls=%async_computation.26 | async-start | bytes 2359296 | tf_op jit(solution)/shard_map/reduce_scatter | solution.py:347
  209.9 174.3 %reduce-scatter.31.cloned.1.call-start = ((), (), s32[]{:S(2)}) async-start(), calls=%async_computation.23 | async-start | bytes 2359296 | tf_op jit(solution)/shard_map/reduce_scatter | solution.py:341
  216.4 238.3 %reduce-scatter.27.cloned.1.call-start = ((), (), s32[]{:S(2)}) async-start(), calls=%async_computation.21 | async-start | bytes 2359296 | tf_op jit(solution)/shard_map/reduce_scatter | solution.py:338
  225.0 276.0 %reduce-scatter.23.cloned.1.call-start = ((), (), s32[]{:S(2)}) async-start(), calls=%async_computation.19 | async-start | bytes 5242880 | tf_op jit(solution)/shard_map/reduce_scatter | solution.py:310
  248.6 299.4 %reduce-scatter.21.cloned.1.call-start = ((), (), s32[]{:S(2)}) async-start(), calls=%async_computation.18 | async-start | bytes 5242880 | tf_op jit(solution)/shard_map/reduce_scatter | solution.py:304
  311.9 328.1 %reduce-scatter.51.cloned.1.call-start = ((), (), s32[]{:S(2)}) async-start(), calls=%async_computation.33 | async-start | bytes 4718592
  336.1 456.2 %reduce-scatter.45.cloned.1.call-start = ((), (), s32[]{:S(2)}) async-start(), calls=%async_computation.30 | async-start | bytes 9437184 | tf_op jit(solution)/shard_map/reduce_scatter | solution.py:353
  350.7 593.7 %reduce-scatter.41.cloned.1.call-start = ((), (), s32[]{:S(2)}) async-start(), calls=%async_computation.28 | async-start | bytes 9437184 | tf_op jit(solution)/shard_map/reduce_scatter | solution.py:350
  361.5 604.3 %reduce-scatter.39.cloned.1.call-start = ((), (), s32[]{:S(2)}) async-start(), calls=%async_computation.27 | async-start | bytes 327680 | tf_op jit(solution)/shard_map/reduce_scatter | solution.py:370
  362.1 626.4 %reduce-scatter.33.cloned.1.call-start = ((), (), s32[]{:S(2)}) async-start(), calls=%async_computation.24 | async-start | bytes 327680 | tf_op jit(solution)/shard_map/reduce_scatter | solution.py:364
  384.2 626.7 %reduce-scatter.29.cloned.1.call-start = ((), (), s32[]{:S(2)}) async-start(), calls=%async_computation.22 | async-start | bytes 327680 | tf_op jit(solution)/shard_map/reduce_scatter | solution.py:361
  454.7 678.1 %reduce-scatter.49.cloned.1.call-start = ((), (), s32[]{:S(2)}) async-start(), calls=%async_computation.32 | async-start | bytes 7077888
  583.5 209.2 %copy-start.47 = (f32[1,1024]{1,0:T(1,128)S(1)}, f32[1,1024]{1,0:T(1,128)}, u32[]{:S(2)}) copy-start(f32[1,1024]{1,0:T(1,128)} %get-tuple-element.191) | copy-start | bytes 12292
  583.5 598.6 %reduce-scatter.35.cloned.1.call-start = ((), (), s32[]{:S(2)}) async-start(), calls=%async_computation.25 | async-start | bytes 655360 | tf_op jit(solution)/shard_map/reduce_scatter | solution.py:367
  644.3 539.7 %reduce-scatter.47.cloned.1.call-start = ((), (), s32[]{:S(2)}) async-start(), calls=%async_computation.31 | async-start | bytes 1310720 | tf_op jit(solution)/shard_map/reduce_scatter | solution.py:376
  792.4 419.1 %reduce-scatter.43.cloned.1.call-start = ((), (), s32[]{:S(2)}) async-start(), calls=%async_computation.29 | async-start | bytes 1310720 | tf_op jit(solution)/shard_map/reduce_scatter | solution.py:373
  792.7 151.9 %copy-start.39 = (f32[1024]{0:T(1024)S(1)}, f32[1024]{0:T(1024)}, u32[]{:S(2)}) copy-start(f32[1024]{0:T(1024)} %get-tuple-element.178) | copy-start | bytes 12292
  792.7 151.9 %copy-start.40 = (f32[1024]{0:T(1024)S(1)}, f32[1024]{0:T(1024)}, u32[]{:S(2)}) copy-start(f32[1024]{0:T(1024)} %get-tuple-element.176) | copy-start | bytes 12292
  944.5 292.8 %reduce-scatter.25.cloned.1.call-start = ((), (), s32[]{:S(2)}) async-start(), calls=%async_computation.20 | async-start | bytes 983040 | tf_op jit(solution)/shard_map/reduce_scatter | solution.py:358
  (53 other events, 1252.2 us)
Sparse Core Ops, SparseCore 0:
  22.7 39.9 all-gather.4
  64.3 34.4 all-gather.2
  205.3 36.0 all-reduce.5
  245.2 68.2 reduce-scatter.36
  317.3 66.8 reduce-scatter.30
  388.0 66.6 reduce-scatter.26
  457.4 43.5 reduce-scatter.22
  503.5 44.4 reduce-scatter.20
  552.1 87.9 reduce-scatter.50
  643.5 148.7 reduce-scatter.44
  796.4 147.9 reduce-scatter.40
  946.8 19.0 reduce-scatter.38
  968.4 20.0 reduce-scatter.32
  990.8 20.0 reduce-scatter.28
  1014.8 117.9 reduce-scatter.48
  1135.9 20.8 reduce-scatter.34
  1159.1 24.7 reduce-scatter.46
  1186.5 24.8 reduce-scatter.42
  1214.0 23.2 reduce-scatter.24
where the time goes:
time: 1250 us
  waiting for transfers between devices  734 us (59%)
  matrix products  233 us (19%)
  local copies, waits for them, and re-layouts  130 us (10%)
  other arithmetic  69.5 us (6%)
  blocking collectives  60.8 us (5%)
  between operations  15.8 us (1%)
    unnamed x22, waiting for transfers between devices  170 us
    reduce_scatter x1, waiting for transfers between devices, body(): lax.psum_scatter(weight_down[None].astype(jnp.bfloat16), 'wide', scatter_...  148 us
    reduce_scatter x1, waiting for transfers between devices, body(): lax.psum_scatter(weight_up[None].astype(jnp.bfloat16), 'wide', scatter_di...  139 us
    unnamed x134, local copies, waits for them, and re-layouts  66.8 us
    reduce_scatter x1, waiting for transfers between devices, body(): lax.psum_scatter(weight_self_out[None].astype(jnp.bfloat16), 'wide', scat...  49.1 us
    reduce_scatter x1, waiting for transfers between devices, body(): lax.psum_scatter(grad_values_self.reshape(item_count, full_len, model_wid...  46 us
    reduce_scatter x1, waiting for transfers between devices, body(): lax.psum_scatter(grad_keys_self.reshape(item_count, full_len, model_width...  44.8 us
    psum x1, blocking collectives, body(): lax.psum((jnp.stack([gain_one, gain_two, gain_three]), jnp.stack([shift_o...  40.6 us
  transfers between devices with their start and end apart: 19, of which 15 were waited for; matrix products, arithmetic and copies ran while one was open for 25% of the time, Pallas kernels for 0%

commit v1 on v0

v1 whole, which is shorter than its diff:
```python
import jax
import jax.numpy as jnp
from jax import lax
from jax.experimental import pallas as pl
from jax.experimental.pallas import tpu as pltpu
from jax.sharding import PartitionSpec as P

HEAD_DIM = 64
PAIR = 2 * HEAD_DIM
SCALE = HEAD_DIM**-0.5
NEG = -1e30
BF = jnp.bfloat16
F32 = jnp.float32
VMEM = 56 * 1024 * 1024


def dot(left, right, left_axis, right_axis):
    return lax.dot_general(
        left, right, (((left_axis,), (right_axis,)), ((), ())), preferred_element_type=F32
    )


def two_heads(rows):
    lane = lax.broadcasted_iota(jnp.int32, rows.shape, 1)
    zero = jnp.zeros_like(rows)
    return jnp.concatenate(
        [jnp.where(lane < HEAD_DIM, rows, zero), jnp.where(lane < HEAD_DIM, zero, rows)], 0
    )


def block_rows(here, block, size):
    return pl.ds(pl.multiple_of((here ^ block) * size, size), size)


def causal_mask(scores, size):
    key = lax.broadcasted_iota(jnp.int32, scores.shape, 0)
    query = lax.broadcasted_iota(jnp.int32, scores.shape, 1)
    return jnp.where(key <= lax.rem(query, size), scores, NEG)


def self_forward_kernel(here_ref, q_ref, k_ref, v_ref, o_ref, log_ref, *, blocks):
    here = here_ref[0]
    size = q_ref.shape[0] // blocks
    for p in range(blocks):
        rows = block_rows(here, p, size)
        queries = two_heads(q_ref[rows, :] * BF(SCALE))
        scores = []
        for j in range(p + 1):
            s = dot(k_ref[block_rows(here, j, size), :], queries, 1, 1)
            scores.append(causal_mask(s, size) if j == p else s)
        top = scores[0].max(0, keepdims=True)
        for s in scores[1:]:
            top = jnp.maximum(top, s.max(0, keepdims=True))
        total = jnp.zeros_like(top)
        mixed = [jnp.zeros((HEAD_DIM, size), F32)] * 2
        for j in range(p + 1):
            e = jnp.exp(scores[j] - top)
            total = total + e.sum(0, keepdims=True)
            low = e.astype(BF)
            values = v_ref[block_rows(here, j, size), :].T
            for h in range(2):
                mixed[h] = mixed[h] + dot(
                    values[h * HEAD_DIM : (h + 1) * HEAD_DIM],
                    low[:, h * size : (h + 1) * size],
                    1,
                    0,
                )
        inverse = 1.0 / total
        both = jnp.concatenate(
            [mixed[h] * inverse[:, h * size : (h + 1) * size] for h in range(2)], 0
        )
        o_ref[rows, :] = both.T.astype(BF)
        log_ref[0, :, 2 * size * p : 2 * size * (p + 1)] = top + jnp.log(total)


def row_dots(left, right):
    product = left.astype(F32).T * right.astype(F32).T
    return jnp.concatenate(
        [product[:HEAD_DIM].sum(0, keepdims=True), product[HEAD_DIM:].sum(0, keepdims=True)], 1
    )


def self_backward_kernel(
    here_ref, q_ref, k_ref, v_ref, o_ref, do_ref, log_ref, dq_ref, dk_ref, dv_ref, *, blocks
):
    here = here_ref[0]
    size = q_ref.shape[0] // blocks
    queries, grads, inner, dq = [], [], [], []
    for p in range(blocks):
        rows = block_rows(here, p, size)
        queries.append(two_heads(q_ref[rows, :] * BF(SCALE)))
        grads.append(two_heads(do_ref[rows, :]))
        inner.append(row_dots(do_ref[rows, :], o_ref[rows, :]))
        dq.append([jnp.zeros((HEAD_DIM, size), F32)] * 2)
    for j in range(blocks):
        rows = block_rows(here, j, size)
        keys, values = k_ref[rows, :], v_ref[rows, :]
        turned = keys.T
        dk = jnp.zeros(keys.shape, F32)
        dv = jnp.zeros(keys.shape, F32)
        for p in range(j, blocks):
            s = dot(keys, queries[p], 1, 1)
            if j == p:
                s = causal_mask(s, size)
            probs = jnp.exp(s - log_ref[0, :, 2 * size * p : 2 * size * (p + 1)])
            dprobs = dot(values, grads[p], 1, 1)
            ds = (probs * (dprobs - inner[p])).astype(BF)
            dv = dv + dot(probs.astype(BF), grads[p], 1, 0)
            dk = dk + dot(ds, queries[p], 1, 0)
            for h in range(2):
                dq[p][h] = dq[p][h] + dot(
                    turned[h * HEAD_DIM : (h + 1) * HEAD_DIM],
                    ds[:, h * size : (h + 1) * size],
                    1,
                    0,
                )
        dk_ref[rows, :] = dk.astype(BF)
        dv_ref[rows, :] = dv.astype(BF)
    for p in range(blocks):
        both = jnp.concatenate(dq[p], 0) * SCALE
        dq_ref[block_rows(here, p, size), :] = both.T.astype(BF)


def pair_spec(rows):
    return pl.BlockSpec((rows, PAIR), lambda i, *_: (0, i))


def log_spec(width):
    return pl.BlockSpec((1, 1, width), lambda i, *_: (i, 0, 0))


def self_forward(here, q, k, v, blocks):
    rows, width = q.shape
    pairs = width // PAIR
    spec = pair_spec(rows)
    return pl.pallas_call(
        lambda *refs: self_forward_kernel(*refs, blocks=blocks),
        name="self_forward",
        out_shape=(
            jax.ShapeDtypeStruct((rows, width), BF),
            jax.ShapeDtypeStruct((pairs, 1, 2 * rows), F32),
        ),
        grid_spec=pltpu.PrefetchScalarGridSpec(
            num_scalar_prefetch=1,
            grid=(pairs,),
            in_specs=[spec] * 3,
            out_specs=(spec, log_spec(2 * rows)),
        ),
        compiler_params=pltpu.CompilerParams(vmem_limit_bytes=VMEM),
        cost_estimate=pl.CostEstimate(
            flops=10 * pairs * rows * rows * PAIR,
            bytes_accessed=8 * rows * width,
            transcendentals=pairs * rows * rows,
        ),
    )(here, q, k, v)


def self_backward(here, q, k, v, o, do, log_total, blocks):
    rows, width = q.shape
    pairs = width // PAIR
    spec = pair_spec(rows)
    return pl.pallas_call(
        lambda *refs: self_backward_kernel(*refs, blocks=blocks),
        name="self_backward",
        out_shape=(jax.ShapeDtypeStruct((rows, width), BF),) * 3,
        grid_spec=pltpu.PrefetchScalarGridSpec(
            num_scalar_prefetch=1,
            grid=(pairs,),
            in_specs=[spec] * 5 + [log_spec(2 * rows)],
            out_specs=(spec,) * 3,
        ),
        compiler_params=pltpu.CompilerParams(vmem_limit_bytes=VMEM),
        cost_estimate=pl.CostEstimate(
            flops=20 * pairs * rows * rows * PAIR,
            bytes_accessed=16 * rows * width,
            transcendentals=pairs * rows * rows,
        ),
    )(here, q, k, v, o, do, log_total)


def cross_forward_kernel(live_ref, q_ref, k_ref, v_ref, o_ref, log_ref):
    size = q_ref.shape[0]
    queries = two_heads(q_ref[...] * BF(SCALE))
    s = dot(k_ref[...], queries, 1, 1)
    s = jnp.where(live_ref[...] > 0, s, NEG)
    top = s.max(0, keepdims=True)
    e = jnp.exp(s - top)
    total = e.sum(0, keepdims=True)
    low = e.astype(BF)
    values = v_ref[...].T
    inverse = 1.0 / total
    both = jnp.concatenate(
        [
            dot(
                values[h * HEAD_DIM : (h + 1) * HEAD_DIM],
                low[:, h * size : (h + 1) * size],
                1,
                0,
            )
            * inverse[:, h * size : (h + 1) * size]
            for h in range(2)
        ],
        0,
    )
    o_ref[...] = both.T.astype(BF)
    log_ref[0] = top + jnp.log(total)


def cross_backward_kernel(
    live_ref, q_ref, k_ref, v_ref, o_ref, do_ref, log_ref, dq_ref, dk_ref, dv_ref
):
    size = q_ref.shape[0]
    queries = two_heads(q_ref[...] * BF(SCALE))
    grads = two_heads(do_ref[...])
    inner = row_dots(do_ref[...], o_ref[...])
    keys = k_ref[...]
    s = dot(keys, queries, 1, 1)
    s = jnp.where(live_ref[...] > 0, s, NEG)
    probs = jnp.exp(s - log_ref[0])
    dprobs = dot(v_ref[...], grads, 1, 1)
    ds = (probs * (dprobs - inner)).astype(BF)
    dv_ref[...] = dot(probs.astype(BF), grads, 1, 0).astype(BF)
    dk_ref[...] = dot(ds, queries, 1, 0).astype(BF)
    turned = keys.T
    both = jnp.concatenate(
        [
            dot(
                turned[h * HEAD_DIM : (h + 1) * HEAD_DIM],
                ds[:, h * size : (h + 1) * size],
                1,
                0,
            )
            for h in range(2)
        ],
        0,
    )
    dq_ref[...] = (both * SCALE).T.astype(BF)


def cross_forward(live, q, k, v):
    rows, width = q.shape
    slots = k.shape[0]
    pairs = width // PAIR
    return pl.pallas_call(
        cross_forward_kernel,
        name="cross_forward",
        out_shape=(
            jax.ShapeDtypeStruct((rows, width), BF),
            jax.ShapeDtypeStruct((pairs, 1, 2 * rows), F32),
        ),
        grid=(pairs,),
        in_specs=[
            pl.BlockSpec((slots, 1), lambda i: (0, 0)),
            pair_spec(rows),
            pair_spec(slots),
            pair_spec(slots),
        ],
        out_specs=(pair_spec(rows), log_spec(2 * rows)),
        compiler_params=pltpu.CompilerParams(vmem_limit_bytes=VMEM),
        cost_estimate=pl.CostEstimate(
            flops=16 * pairs * rows * slots * PAIR,
            bytes_accessed=4 * (rows + slots) * width,
            transcendentals=2 * pairs * rows * slots,
        ),
    )(live, q, k, v)


def cross_backward(live, q, k, v, o, do, log_total):
    rows, width = q.shape
    slots = k.shape[0]
    pairs = width // PAIR
    return pl.pallas_call(
        cross_backward_kernel,
        name="cross_backward",
        out_shape=(
            jax.ShapeDtypeStruct((rows, width), BF),
            jax.ShapeDtypeStruct((slots, width), BF),
            jax.ShapeDtypeStruct((slots, width), BF),
        ),
        grid=(pairs,),
        in_specs=[
            pl.BlockSpec((slots, 1), lambda i: (0, 0)),
            pair_spec(rows),
            pair_spec(slots),
            pair_spec(slots),
            pair_spec(rows),
            pair_spec(rows),
            log_spec(2 * rows),
        ],
        out_specs=(pair_spec(rows), pair_spec(slots), pair_spec(slots)),
        compiler_params=pltpu.CompilerParams(vmem_limit_bytes=VMEM),
        cost_estimate=pl.CostEstimate(
            flops=40 * pairs * rows * slots * PAIR,
            bytes_accessed=8 * (rows + slots) * width,
            transcendentals=2 * pairs * rows * slots,
        ),
    )(live, q, k, v, o, do, log_total)


def standardize(rows):
    centered = rows - jnp.mean(rows, -1, keepdims=True)
    inverse = lax.rsqrt(jnp.mean(centered * centered, -1, keepdims=True) + 1e-05)
    return centered * inverse, inverse


def norm_back(grad_out, gain, unit_rows, inverse):
    grad_unit = grad_out * gain
    grad_in = inverse * (
        grad_unit
        - jnp.mean(grad_unit, -1, keepdims=True)
        - unit_rows * jnp.mean(grad_unit * unit_rows, -1, keepdims=True)
    )
    return grad_in, jnp.sum(grad_out * unit_rows, 0), jnp.sum(grad_out, 0)


def gelu_and_slope(pre):
    square = pre * pre
    bend = jnp.tanh(0.7978845608028654 * pre * (1.0 + 0.044715 * square))
    half = 0.5 * (1.0 + bend)
    slope = half + 0.5 * pre * (1.0 - bend * bend) * (
        0.7978845608028654 * (1.0 + 3.0 * 0.044715 * square)
    )
    return pre * half, slope


def body(
    image_tokens,
    text_states,
    caption_lengths,
    text_mask,
    self_qkv,
    self_out,
    cross_query,
    cross_kv,
    cross_out,
    mlp_in,
    mlp_out,
    norm_gains,
    norm_shifts,
    out_biases,
    mlp_bias,
    cotangent,
):
    _, block, width = image_tokens.shape
    blocks = lax.axis_size("narrow")
    wide_size = lax.axis_size("wide")
    here = lax.axis_index("narrow")
    line = lax.axis_index("wide")
    chip, core = here // 2, here % 2
    wide_bits = wide_size.bit_length() - 1
    mates = [(i, i ^ 1) for i in range(blocks)]
    across = [(i, i ^ 2) for i in range(blocks)]

    def to_mate(value):
        return lax.ppermute(value, "narrow", mates)

    def to_chip(value):
        return lax.ppermute(value, "narrow", across)

    def item(array, index):
        return lax.dynamic_index_in_dim(array, index, 0, keepdims=False)

    def woven(own, other):
        half = own.shape[0] // 2
        return jnp.concatenate([own[:half], other[:half], own[half:], other[half:]], 0)

    def columns(array, side):
        quarter = array.shape[-1] // 4
        return jnp.concatenate(
            [
                lax.dynamic_slice_in_dim(array, (2 * k + side) * quarter, quarter, array.ndim - 1)
                for k in range(2)
            ],
            -1,
        )

    def chosen(first, second):
        return jnp.where(core == 0, first, second), jnp.where(core == 0, second, first)

    def exchange(value, axis):
        if axis == "x":
            return to_chip(value)
        return lax.ppermute(value, "wide", [(i, i ^ (1 << axis)) for i in range(wide_size)])

    def scatter_sum(partial, order):
        rows, cols = partial.shape
        held = [partial.reshape((2,) * wide_bits + (rows // wide_size, cols))]

        def take(value, axis, mine):
            bit = chip if axis == "x" else (line >> axis) & 1
            bit = bit if mine else 1 - bit
            if axis == "x":
                return lax.dynamic_slice_in_dim(value, bit * (cols // 2), cols // 2, value.ndim - 1)
            return lax.dynamic_slice_in_dim(value, bit, 1, wide_bits - 1 - axis)

        for axis in order:
            sent = sum(take(h, axis, False).astype(F32) for h in held).astype(BF)
            held = [take(h, axis, True) for h in held] + [exchange(sent, axis)]
        total = sum(h.astype(F32) for h in held)
        return total.reshape(rows // wide_size, cols // 2)

    near = list(range(wide_bits))
    order_x = ["x"] + near
    order_y = near[:1] + ["x"] + near[1:]
    order_z = near[1:] + near[:1] + ["x"]

    def weight_grad(left, right, order):
        return scatter_sum(dot(left, right, 0, 0).astype(BF), order)

    x_own = item(image_tokens, chip)
    x_far = to_chip(item(image_tokens, 1 - chip))
    x_mate = to_mate(x_own)
    x_mate_far = to_mate(x_far)
    text_own = item(text_states, chip)
    text_far = to_chip(item(text_states, 1 - chip))
    text_two = jnp.concatenate([text_own, text_far], 0)
    text_all = jnp.concatenate(chosen(text_two, to_mate(text_two)), 0)
    slot_block = text_own.shape[0]
    slots = slot_block * blocks
    slot_order = jnp.stack([(2 * chip) ^ k for k in (0, 2, 1, 3)])
    slot = (slot_order[:, None] * slot_block + jnp.arange(slot_block)[None, :]).reshape(slots)
    kept = item(text_mask, chip).reshape(blocks, slot_block)
    kept = jnp.concatenate([item(kept, (2 * chip) ^ k) for k in (0, 2, 1, 3)], 0)
    length = item(caption_lengths, chip)
    live = ((slot < length) & ((kept == 1) | (slot == 0))).astype(F32).reshape(slots, 1)
    cot_own = item(cotangent, chip)
    cot_far = to_chip(item(cotangent, 1 - chip))
    e3 = jnp.concatenate([cot_own, cot_far], 0)

    x = jnp.concatenate([x_own, x_far], 0).astype(F32)
    x_full = jnp.concatenate([x_own, x_mate, x_far, x_mate_far], 0).astype(F32)
    unit_full, _ = standardize(x_full)
    a_full = (unit_full * norm_gains[0] + norm_shifts[0]).astype(BF)

    w_qkv_own, w_qkv_mate = columns(self_qkv, core), columns(self_qkv, 1 - core)
    def head_rows(side):
        quarter = width // 4
        return jnp.concatenate(
            [
                lax.dynamic_slice_in_dim(self_out, (2 * k + side) * quarter, quarter, 0)
                for k in range(2)
            ],
            0,
        )

    w_out_own, w_out_mate = head_rows(core), head_rows(1 - core)

    q, k, v = (dot(a_full, w_qkv_own[j], 1, 0).astype(BF) for j in range(3))
    place = here.reshape(1).astype(jnp.int32)
    os_heads, log_self = self_forward(place, q, k, v, blocks)

    def own_rows(array):
        return jnp.concatenate([array[:block], array[2 * block : 3 * block]], 0)

    def mate_rows(array):
        return jnp.concatenate([array[block : 2 * block], array[3 * block :]], 0)

    os_own = own_rows(os_heads)
    os_other = to_mate(mate_rows(os_heads))
    h1 = (
        x
        + dot(os_own, w_out_own, 1, 0)
        + dot(os_other, w_out_mate, 1, 0)
        + out_biases[0]
    )
    first, second = chosen(os_own, os_other)
    half = width // 4
    os_rows = jnp.concatenate([first[:, :half], second[:, :half], first[:, half:], second[:, half:]], 1)
    os_full = woven(os_rows, to_mate(os_rows))

    unit_two, inverse_two = standardize(h1)
    c = (unit_two * norm_gains[1] + norm_shifts[1]).astype(BF)
    qc = dot(c, cross_query, 1, 0).astype(BF)
    tk = dot(text_all, cross_kv[0], 1, 0).astype(BF)
    tv = dot(text_all, cross_kv[1], 1, 0).astype(BF)
    oc, log_cross = cross_forward(live, qc, tk, tv)
    h2 = h1 + dot(oc, cross_out, 1, 0) + out_biases[1]
    c_full = woven(c, to_mate(c))
    oc_full = woven(oc, to_mate(oc))

    unit_three, inverse_three = standardize(h2)
    m = (unit_three * norm_gains[2] + norm_shifts[2]).astype(BF)
    m_full = woven(m, to_mate(m))
    g, slope = gelu_and_slope(dot(m, mlp_in, 1, 0) + mlp_bias)
    g, slope = g.astype(BF), slope.astype(BF)
    g_full = woven(g, to_mate(g))
    layer_out = h2 + dot(g, mlp_out, 1, 0) + out_biases[2]

    e3_cols = woven(columns(e3, core), to_mate(columns(e3, 1 - core)))
    part_down = weight_grad(g_full, e3_cols, order_y)
    dpre = (dot(e3, mlp_out, 1, 1).astype(BF).astype(F32) * slope.astype(F32)).astype(BF)
    dpre_cols = woven(columns(dpre, core), to_mate(columns(dpre, 1 - core)))
    part_up = weight_grad(m_full, dpre_cols, order_z)
    grad_three, gain_three, shift_three = norm_back(
        dot(dpre, mlp_in, 1, 1), norm_gains[2], unit_three, inverse_three
    )
    e2 = e3.astype(F32) + grad_three
    f2 = e2.astype(BF)

    f2_cols = woven(columns(f2, core), to_mate(columns(f2, 1 - core)))
    part_cout = weight_grad(oc_full, f2_cols, order_x)
    doc = dot(f2, cross_out, 1, 1).astype(BF)
    dqc, dtk, dtv = cross_backward(live, qc, tk, tv, oc, doc, log_cross)
    dt = jnp.stack([dtk, dtv])
    dt = (dt.astype(F32) + to_mate(dt).astype(F32)).astype(BF)
    part_ckv = [
        weight_grad(text_all, columns(dt[j], core), order) for j, order in ((0, order_x), (1, order_z))
    ]
    dt_own = lax.dynamic_slice_in_dim(dt, core * 2 * slot_block, 2 * slot_block, 1)
    grad_text = dot(dt_own[0], cross_kv[0], 1, 1) + dot(dt_own[1], cross_kv[1], 1, 1)
    dqc_cols = woven(columns(dqc, core), to_mate(columns(dqc, 1 - core)))
    part_cq = weight_grad(c_full, dqc_cols, order_y)
    grad_two, gain_two, shift_two = norm_back(
        dot(dqc, cross_query, 1, 1), norm_gains[1], unit_two, inverse_two
    )
    e1 = e2 + grad_two
    f1 = e1.astype(BF)

    do_own = dot(f1, w_out_own, 1, 1).astype(BF)
    do_far = to_mate(dot(f1, w_out_mate, 1, 1).astype(BF))
    do_heads = woven(do_own, do_far)
    dq, dk, dv = self_backward(place, q, k, v, os_heads, do_heads, log_self, blocks)
    d_other = to_mate(jnp.stack([mate_rows(d) for d in (dq, dk, dv)]))
    part_qkv = [
        weight_grad(a_full, d, order)
        for d, order in ((dq, order_x), (dk, order_y), (dv, order_z))
    ]
    f1_cols = woven(columns(f1, core), to_mate(columns(f1, 1 - core)))
    part_sout = weight_grad(os_full, f1_cols, order_y)
    grad_a = sum(dot(own_rows(d), w_qkv_own[j], 1, 1) for j, d in enumerate((dq, dk, dv)))
    grad_a = grad_a + sum(dot(d_other[j], w_qkv_mate[j], 1, 1) for j in range(3))
    unit_one, inverse_one = standardize(x)
    grad_one, gain_one, shift_one = norm_back(grad_a, norm_gains[0], unit_one, inverse_one)
    grad_rows = e1 + grad_one

    def home(rows):
        half = rows.shape[0] // 2
        own, far = rows[:half], to_chip(rows[half:].astype(BF)).astype(F32)
        return jnp.stack([jnp.where(chip == 0, own, far), jnp.where(chip == 0, far, own)])

    def column_sum(rows):
        return jnp.sum(rows.astype(F32), 0)

    def all_sum(value):
        value = value + to_mate(value)
        value = value + to_chip(value)
        for bit in near:
            value = value + exchange(value, bit)
        return value

    early = all_sum(
        jnp.concatenate(
            [
                jnp.stack(
                    [gain_two, gain_three, shift_two, shift_three]
                    + [column_sum(v) for v in (f1, f2, e3)]
                ),
                column_sum(dpre).reshape(-1, width),
            ]
        )
    )
    late = all_sum(jnp.stack([gain_one, shift_one]))
    gains = jnp.stack([late[0], early[0], early[1]])
    shifts = jnp.stack([late[1], early[2], early[3]])
    return (
        home(layer_out),
        home(grad_rows),
        home(grad_text),
        jnp.stack(part_qkv),
        part_sout,
        part_cq,
        jnp.stack(part_ckv),
        part_cout,
        part_up,
        part_down,
        gains,
        shifts,
        early[4:7],
        early[7:].reshape(-1),
    )


def solution(mesh):
    rows = P("wide", "narrow", None)
    whole = P()
    return jax.shard_map(
        body,
        mesh=mesh,
        in_specs=(rows, rows, P("wide"), P("wide", None)) + (whole,) * 11 + (rows,),
        out_specs=(rows,) * 3
        + (
            P(None, "wide", "narrow"),
            P("wide", "narrow"),
            P("wide", "narrow"),
            P(None, "wide", "narrow"),
        )
        + (P("wide", "narrow"),) * 3
        + (whole,) * 4,
        check_vma=False,
    )
```

time: 1250 us -> 538 us (0.43)
  waiting for transfers between devices: 734 us -> 193 us
  matrix products: 233 us -> 95 us
  starting transfers between devices: 2.34 us -> 82.3 us
  local copies, waits for them, and re-layouts: 130 us -> 62.2 us
  blocking collectives: 60.8 us -> 0 us
  Pallas kernels: 0 us -> 46.6 us
  other arithmetic: 69.5 us -> 51 us
  between operations: 15.8 us -> 2.84 us
    reduce_scatter x14 -> x0, waiting for transfers between devices: 558 us -> none  [the longest x1 148 us: body(): lax.psum_scatter(weight_down[None].astype(jnp.bfloat16), 'wide', scatter_...]
    ppermute x0 -> x73, waiting for transfers between devices: none -> 193 us  [the longest x36 144 us: exchange(): lax.ppermute(value, 'wide', [(i, i ^ 1 << axis) for i in range(wide_size)])]
    unnamed x22 -> x0, waiting for transfers between devices: 170 us -> none
    dot_general x33 -> x35, matrix products: 233 us -> 95 us  [dot(): lax.dot_general(left, right, (((left_axis,), (right_axis,)), ((), ())), p...]
    ppermute x0 -> x73, starting transfers between devices: none -> 82.3 us  [the longest x36 57.7 us: exchange(): lax.ppermute(value, 'wide', [(i, i ^ 1 << axis) for i in range(wide_size)])]
    unnamed x134 -> x250, local copies, waits for them, and re-layouts: 66.8 us -> 12.1 us
    pallas_call x0 -> x4, Pallas kernels: none -> 46.6 us  [the longest x1 18.2 us: self_backward(): pl.pallas_call(lambda *refs: self_backward_kernel(*refs, blocks=blocks),...]
    psum x1 -> x0, blocking collectives: 40.6 us -> none  [body(): lax.psum((jnp.stack([gain_one, gain_two, gain_three]), jnp.stack([shift_o...]
  transfers between devices with their start and end apart: 19 -> 73, of which waited for: 15 -> 36; matrix products, arithmetic and copies ran while one was open for 25% -> 27% of each run, Pallas kernels for 0% -> 6%
where the time goes in v1:
time: 538 us; the launch traced here: 533 us
  waiting for transfers between devices  193 us (36%)
  matrix products  95 us (18%)
  starting transfers between devices  82.3 us (15%)
  local copies, waits for them, and re-layouts  62.2 us (12%)
  other arithmetic  51 us (9%)
  Pallas kernels  46.6 us (9%)
    ppermute x36, waiting for transfers between devices, exchange(): lax.ppermute(value, 'wide', [(i, i ^ 1 << axis) for i in range(wide_size)])  144 us
    dot_general x35, matrix products, dot(): lax.dot_general(left, right, (((left_axis,), (right_axis,)), ((), ())), p...  95 us
    ppermute x36, starting transfers between devices, exchange(): lax.ppermute(value, 'wide', [(i, i ^ 1 << axis) for i in range(wide_size)])  57.7 us
    ppermute x18, waiting for transfers between devices, to_chip(): return lax.ppermute(value, 'narrow', across)  47.5 us
    ppermute x18, starting transfers between devices, to_chip(): return lax.ppermute(value, 'narrow', across)  21.4 us
    pallas_call x1, Pallas kernels, self_backward(): pl.pallas_call(lambda *refs: self_backward_kernel(*refs, blocks=blocks),...  18.2 us
    slice x11, local copies, waits for them, and re-layouts, woven(): other[:half]  12.8 us
    unnamed x250, local copies, waits for them, and re-layouts  12.1 us
  transfers between devices with their start and end apart: 73, of which 36 were waited for; matrix products, arithmetic and copies ran while one was open for 27% of the time, Pallas kernels for 6%

profile of v1, /device:TPU:0, one launch (start us, length us, event | category | flops | bytes accessed | tf_op | source)
XLA Modules:
  0.0 532.6 jit_solution(16052715102627617246)
XLA Ops:
  12.3 5.7 %constant_dynamic-slice_fusion.26 = (bf16[3,1024,256]{2,1,0:T(8,128)(2,1)}, bf16[3,1024,256]{2,1,0:T(8,128)(2,1)}, bf16[3,1024,256]{2,1,0:T(8,128)(2,1)}, bf16[3,1024,256]{2,1,0:T(8,128)(2,1)}) fusion(bf16[3,1024,1024]{2,1,0:T(8,128)(2,1)} %param.20, s32[]{:T(128)S(6)} %select_n.158, s32[]{:T(128)S(6)} %select_n.156, s32[]{:T(128)S(6)} %select_n.155, ...), kind=kLoop, calls=%fused_computation.389 | loop fusion | bytes 12582928 | tf_op jit(solution)/shard_map/dynamic_slice | solution.py:371
  25.8 5.0 collective-permute-done.7
  49.1 12.0 %self_forward.1 = (bf16[1024,512]{1,0:T(8,128)(2,1)}, f32[4,1,2048]{2,1,0:T(1,128)}) custom-call(s32[1]{0:T(128)} %bitcast.2.refs_0_, bf16[1024,512]{1,0:T(8,128)(2,1)} %convolution_convert_fusion.10.refs_1_, bf16[1024,512]{1,0:T(8,128)(2,1)} %convolution_convert_fusion.9.refs_2_, bf16[1024,512]{1,0:T(8,128)(2,1)} %convolution_convert_fusion.8.refs_3_), custom_call_target="tpu_custom_call" | custom-call | flops 5368709120 | bytes 4194304 | tf_op jit(solution)/shard_map/self_forward/pallas_call | solution.py:136
  71.4 7.6 %cross_forward.1 = (bf16[512,1024]{1,0:T(8,128)(2,1)}, f32[8,1,1024]{2,1,0:T(1,128)}) custom-call(f32[128,1]{1,0:T(8,128)} %and_convert_fusion.live_ref, bf16[512,1024]{1,0:T(8,128)(2,1)} %convolution_convert_fusion.7.q_ref, bf16[128,1024]{1,0:T(8,128)(2,1)} %fusion.104.k_ref, bf16[128,1024]{1,0:T(8,128)(2,1)} %fusion.107.v_ref), custom_call_target="tpu_custom_call" | custom-call | flops 1073741824 | bytes 2621440 | tf_op jit(solution)/shard_map/cross_forward/pallas_call | solution.py:244
  82.7 12.9 %multiply_convert_fusion.1 = (bf16[512,4096]{1,0:T(8,128)(2,1)}, f32[512,4096]{1,0:T(8,128)}) fusion(f32[4096]{0:T(1024)S(1)} %copy-done.121, bf16[512,1024]{1,0:T(8,128)(2,1)S(1)} %add_convert_fusion.3, bf16[1024,4096]{1,0:T(8,128)(2,1)} %param.25), kind=kOutput, calls=%fused_computation.13 | convolution fusion | flops 4315938816 | bytes 22036480 | tf_op jit(solution)/shard_map/dot_general | solution.py:18
  95.7 12.5 %convert_reduce_fusion = (f32[4096]{0:T(1024)S(1)}, bf16[512,4096]{1,0:T(8,128)(2,1)S(1)}) fusion(f32[512,4096]{1,0:T(8,128)} %get-tuple-element.181, f32[4096]{0:T(1024)S(1)} %copy-done.121, bf16[4096,1024]{1,0:T(8,128)(2,1)} %param.26, bf16[256,1024]{1,0:T(8,128)(2,1)} %collective-permute-done.7, bf16[256,1024]{1,0:T(8,128)(2,1)S(1)} %copy-done.14), kind=kOutput, calls=%fused_computation.10 | convolution fusion | flops 4349489152 | bytes 22052864 | tf_op jit(solution)/shard_map/dot_general | solution.py:18
  108.2 9.1 %multiply_reduce_fusion = (f32[1024]{0:T(1024)S(1)}, f32[512]{0:T(512)S(1)}, f32[512]{0:T(512)S(1)}, f32[1024]{0:T(1024)S(1)}, f32[512,1024]{1,0:T(8,128)S(1)}) fusion(f32[512,1024]{1,0:T(8,128)S(1)} %get-tuple-element.179, f32[512]{0:T(512)S(1)} %add_rsqrt_fusion.2, f32[512]{0:T(512)S(1)} %broadcast_multiply_fusion.8, f32[1024]{0:T(1024)S(1)} %bitcast.259, ...), kind=kOutput, calls=%fused_computation.118 | convolution fusion | flops 4299682816 | bytes 16797696 | tf_op jit(solution)/shard_map/dot_general | solution.py:18
  121.5 8.7 %cross_backward.1 = (bf16[512,1024]{1,0:T(8,128)(2,1)}, bf16[128,1024]{1,0:T(8,128)(2,1)}, bf16[128,1024]{1,0:T(8,128)(2,1)}) custom-call(f32[128,1]{1,0:T(8,128)} %and_convert_fusion.live_ref, bf16[512,1024]{1,0:T(8,128)(2,1)} %convolution_convert_fusion.7.q_ref, bf16[128,1024]{1,0:T(8,128)(2,1)} %fusion.104.k_ref, bf16[128,1024]{1,0:T(8,128)(2,1)} %fusion.107.v_ref, ...), custom_call_target="tpu_custom_call" | custom-call | flops 2684354560 | bytes 5242880 | tf_op jit(solution)/shard_map/cross_backward/pallas_call | solution.py:272
  137.3 4.7 fusion.259
  155.5 8.3 %add_add_fusion.1 = f32[512,1024]{1,0:T(8,128)S(1)} fusion(f32[512,1024]{1,0:T(8,128)S(1)} %copy-done.13, bf16[512,4096]{1,0:T(8,128)(2,1)} %get-tuple-element.180, bf16[4096,1024]{1,0:T(8,128)(2,1)} %param.26, f32[1024]{0:T(1024)S(1)} %bitcast.272), kind=kOutput, calls=%fused_computation.126 | convolution fusion | flops 4296015872 | bytes 16781312 | tf_op jit(solution)/shard_map/dot_general | solution.py:18
  192.1 18.2 %self_backward.1 = (bf16[1024,512]{1,0:T(8,128)(2,1)}, bf16[1024,512]{1,0:T(8,128)(2,1)}, bf16[1024,512]{1,0:T(8,128)(2,1)}) custom-call(s32[1]{0:T(128)} %bitcast.2.refs_0_, bf16[1024,512]{1,0:T(8,128)(2,1)} %convolution_convert_fusion.10.refs_1_, bf16[1024,512]{1,0:T(8,128)(2,1)} %convolution_convert_fusion.9.refs_2_, ...), custom_call_target="tpu_custom_call" | custom-call | flops 10737418240 | bytes 8388608 | tf_op jit(solution)/shard_map/self_backward/pallas_call | solution.py:162
  227.8 10.8 %collective-permute-done.6 = bf16[256,1024]{1,0:T(8,128)(2,1)S(1)} collective-permute-done((bf16[256,1024]{1,0:T(8,128)(2,1)S(1)}, bf16[256,1024]{1,0:T(8,128)(2,1)S(1)}, u32[]{:S(2)}, u32[]{:S(2)}) %collective-permute-start.6) | collective-permute-done | bytes 524320 | tf_op jit(solution)/shard_map/ppermute | solution.py:358
  262.5 9.0 %collective-permute-done.13 = bf16[2,2,2,128,256]{4,3,2,1,0:T(8,128)(2,1)S(1)} collective-permute-done((bf16[2,2,2,128,256]{4,3,2,1,0:T(8,128)(2,1)S(1)}, bf16[2,2,2,128,256]{4,3,2,1,0:T(8,128)(2,1)S(1)}, u32[]{:S(2)}, u32[]{:S(2)}) %collective-permute-start.13) | collective-permute-done | bytes 524320 | tf_op jit(solution)/shard_map/ppermute | solution.py:358
  277.9 7.1 %collective-permute-done.21 = bf16[2,1,2,128,512]{4,3,2,1,0:T(8,128)(2,1)S(1)} collective-permute-done((bf16[2,1,2,128,512]{4,3,2,1,0:T(8,128)(2,1)S(1)}, bf16[2,1,2,128,512]{4,3,2,1,0:T(8,128)(2,1)S(1)}, u32[]{:S(2)}, u32[]{:S(2)}) %collective-permute-start.21) | collective-permute-done | bytes 524320 | tf_op jit(solution)/shard_map/ppermute | solution.py:383
  295.1 12.4 %collective-permute-done.42 = bf16[1,1,2,128,512]{4,3,2,1,0:T(8,128)(2,1)S(1)} collective-permute-done((bf16[1,1,2,128,512]{4,3,2,1,0:T(8,128)(2,1)S(1)}, bf16[1,1,2,128,512]{4,3,2,1,0:T(8,128)(2,1)S(1)}, u32[]{:S(2)}, u32[]{:S(2)}) %collective-permute-start.42) | collective-permute-done | bytes 262176 | tf_op jit(solution)/shard_map/ppermute | solution.py:383
  307.5 4.5 collective-permute-done.22
  355.3 5.3 collective-permute-done.27
  383.2 4.6 fusion.34
  396.5 4.8 fusion.260
  401.2 8.9 %fusion.11 = bf16[4096,512]{1,0:T(8,128)(2,1)} fusion(bf16[256,4096]{1,0:T(8,128)(2,1)} %get-tuple-element.59, bf16[256,4096]{1,0:T(8,128)(2,1)} %get-tuple-element.57, bf16[256,4096]{1,0:T(8,128)(2,1)} %get-tuple-element.58, bf16[256,4096]{1,0:T(8,128)(2,1)} %get-tuple-element.56, bf16[512,256]{1,0:T(8,128)(2,1)} %copy-done.34, ...), kind=kOutput, calls=%fused_computation.20 | convolution fusion | flops 4338483200 | bytes 13893632 | tf_op jit(solution)/shard_map/dot_general | solution.py:18
  421.8 33.4 %collective-permute-done.65 = f32[2,1024]{1,0:T(2,128)S(1)} collective-permute-done((f32[2,1024]{1,0:T(2,128)S(1)}, f32[2,1024]{1,0:T(2,128)S(1)}, u32[]{:S(2)}, u32[]{:S(2)}) %collective-permute-start.65) | collective-permute-done | bytes 8224 | tf_op jit(solution)/shard_map/ppermute | solution.py:383
  463.5 37.0 %collective-permute-done.67 = f32[2,1024]{1,0:T(2,128)S(1)} collective-permute-done((f32[2,1024]{1,0:T(2,128)S(1)}, f32[2,1024]{1,0:T(2,128)S(1)}, u32[]{:S(2)}, u32[]{:S(2)}) %collective-permute-start.67) | collective-permute-done | bytes 8224 | tf_op jit(solution)/shard_map/ppermute | solution.py:383
  504.7 10.6 %collective-permute-done.55 = bf16[1,1,1,128,2048]{4,3,2,1,0:T(8,128)(2,1)S(1)} collective-permute-done((bf16[1,1,1,128,2048]{4,3,2,1,0:T(8,128)(2,1)S(1)}, bf16[1,1,1,128,2048]{4,3,2,1,0:T(8,128)(2,1)S(1)}, u32[]{:S(2)}, u32[]{:S(2)}) %collective-permute-start.55) | collective-permute-done | bytes 524320 | tf_op jit(solution)/shard_map/ppermute | solution.py:383
  524.4 6.9 %collective-permute-done.62 = bf16[1,1,1,512,256]{4,3,2,1,0:T(8,128)(2,1)S(1)} collective-permute-done((bf16[1,1,1,512,256]{4,3,2,1,0:T(8,128)(2,1)S(1)}, bf16[1,1,1,512,256]{4,3,2,1,0:T(8,128)(2,1)S(1)}, u32[]{:S(2)}, u32[]{:S(2)}) %collective-permute-start.62) | collective-permute-done | bytes 262176 | tf_op jit(solution)/shard_map/ppermute | solution.py:383
  (585 shorter events, 269.9 us)
Async XLA Ops:
  3.0 29.9 %collective-permute-start = (bf16[256,1024]{1,0:T(8,128)(2,1)}, bf16[256,1024]{1,0:T(8,128)(2,1)S(1)}, u32[]{:S(2)}, u32[]{:S(2)}) collective-permute-start(bf16[256,1024]{1,0:T(8,128)(2,1)} %get-tuple-element.128), channel_id=1, source_target_pairs={{0,2},{1,3},{2,0},{3,1},{4,6},{5,7},{6,4},{7,5},{8,10},{9,11},{10,... | collective-permute-start | bytes 1572872 | tf_op jit(solution)/shard_map/ppermute | solution.py:358
  5.9 28.8 %collective-permute-start.1 = (bf16[256,1024]{1,0:T(8,128)(2,1)S(1)}, bf16[256,1024]{1,0:T(8,128)(2,1)}, u32[]{:S(2)}, u32[]{:S(2)}) collective-permute-start(bf16[256,1024]{1,0:T(8,128)(2,1)S(1)} %get-tuple-element.127), channel_id=1, source_target_pairs={{0,1},{1,0},{2,3},{3,2},{4,5},{5,4},{6,7},{7,6},{8,9},{9,8},{10,11... | collective-permute-start | bytes 1572872 | tf_op jit(solution)/shard_map/ppermute | solution.py:355
  7.1 23.7 %collective-permute-start.7 = (bf16[256,1024]{1,0:T(8,128)(2,1)}, bf16[256,1024]{1,0:T(8,128)(2,1)}, u32[]{:S(2)}, u32[]{:S(2)}) collective-permute-start(bf16[256,1024]{1,0:T(8,128)(2,1)} %get-tuple-element.122), channel_id=1, source_target_pairs={{0,2},{1,3},{2,0},{3,1},{4,6},{5,7},{6,4},{7,5},{8,10},{9,11},{10,... | collective-permute-start | bytes 1572872 | tf_op jit(solution)/shard_map/ppermute | solution.py:358
  32.9 31.4 %collective-permute-start.58 = (bf16[512,512]{1,0:T(8,128)(2,1)}, bf16[512,512]{1,0:T(8,128)(2,1)}, u32[]{:S(2)}, u32[]{:S(2)}) collective-permute-start(bf16[512,512]{1,0:T(8,128)(2,1)} %pad_maximum_fusion.25), channel_id=1, source_target_pairs={{0,1},{1,0},{2,3},{3,2},{4,5},{5,4},{6,7},{7,6},{8,9},{9,8},{10,11... | collective-permute-start | bytes 1572872 | tf_op jit(solution)/shard_map/ppermute | solution.py:355
  136.9 259.6 %collective-permute-start.57 = (bf16[512,4096]{1,0:T(8,128)(2,1)}, bf16[512,4096]{1,0:T(8,128)(2,1)}, u32[]{:S(2)}, u32[]{:S(2)}) collective-permute-start(bf16[512,4096]{1,0:T(8,128)(2,1)} %get-tuple-element.180), channel_id=1, source_target_pairs={{0,1},{1,0},{2,3},{3,2},{4,5},{5,4},{6,7},{7,6},{8,9},{9,8},{10,11... | collective-permute-start | bytes 12582920 | tf_op jit(solution)/shard_map/ppermute | solution.py:355
  142.0 131.3 %collective-permute-start.51 = (bf16[512,1024]{1,0:T(8,128)(2,1)S(1)}, bf16[512,1024]{1,0:T(8,128)(2,1)}, u32[]{:S(2)}, u32[]{:S(2)}) collective-permute-start(bf16[512,1024]{1,0:T(8,128)(2,1)S(1)} %add_convert_fusion.3), channel_id=1, source_target_pairs={{0,1},{1,0},{2,3},{3,2},{4,5},{5,4},{6,7},{7,6},{8,9},{9,8},{10,11... | collective-permute-start | bytes 3145736 | tf_op jit(solution)/shard_map/ppermute | solution.py:355
  144.5 101.3 %collective-permute-start.45 = (bf16[512,1024]{1,0:T(8,128)(2,1)}, bf16[512,1024]{1,0:T(8,128)(2,1)}, u32[]{:S(2)}, u32[]{:S(2)}) collective-permute-start(bf16[512,1024]{1,0:T(8,128)(2,1)} %get-tuple-element.25.o_ref), channel_id=1, source_target_pairs={{0,1},{1,0},{2,3},{3,2},{4,5},{5,4},{6,7},{7,6},{8,9},{9,8},{10,11... | collective-permute-start | bytes 3145736 | tf_op jit(solution)/shard_map/ppermute | solution.py:355
  150.9 38.5 %collective-permute-start.8 = (bf16[512,512]{1,0:T(8,128)(2,1)}, bf16[512,512]{1,0:T(8,128)(2,1)}, u32[]{:S(2)}, u32[]{:S(2)}) collective-permute-start(bf16[512,512]{1,0:T(8,128)(2,1)} %convolution_convert_fusion.11), channel_id=1, source_target_pairs={{0,1},{1,0},{2,3},{3,2},{4,5},{5,4},{6,7},{7,6},{8,9},{9,8},{10,11... | collective-permute-start | bytes 1572872 | tf_op jit(solution)/shard_map/ppermute | solution.py:355
  188.1 60.6 %collective-permute-start.31 = (bf16[512,1024]{1,0:T(8,128)(2,1)S(1)}, bf16[512,1024]{1,0:T(8,128)(2,1)}, u32[]{:S(2)}, u32[]{:S(2)}) collective-permute-start(bf16[512,1024]{1,0:T(8,128)(2,1)S(1)} %copy-done.22), channel_id=1, source_target_pairs={{0,1},{1,0},{2,3},{3,2},{4,5},{5,4},{6,7},{7,6},{8,9},{9,8},{10,11... | collective-permute-start | bytes 3145736 | tf_op jit(solution)/shard_map/ppermute | solution.py:355
  189.4 22.9 %collective-permute-start.11 = (bf16[2,128,1024]{2,1,0:T(8,128)(2,1)}, bf16[2,128,1024]{2,1,0:T(8,128)(2,1)S(1)}, u32[]{:S(2)}, u32[]{:S(2)}) collective-permute-start(bf16[2,128,1024]{2,1,0:T(8,128)(2,1)} %pad_maximum_fusion.21), channel_id=1, source_target_pairs={{0,1},{1,0},{2,3},{3,2},{4,5},{5,4},{6,7},{7,6},{8,9},{9,8},{10,11... | collective-permute-start | bytes 1572872 | tf_op jit(solution)/shard_map/ppermute | solution.py:355
  248.7 26.9 %collective-permute-start.41 = (bf16[2,1,2,128,512]{4,3,2,1,0:T(8,128)(2,1)S(1)}, bf16[2,1,2,128,512]{4,3,2,1,0:T(8,128)(2,1)S(1)}, u32[]{:S(2)}, u32[]{:S(2)}) collective-permute-start(bf16[2,1,2,128,512]{4,3,2,1,0:T(8,128)(2,1)S(1)} %constant_dynamic-slice_fusion.23), channel_id=1, source_target_pairs={{0,8},{4,12},{8,0},{12,4},{16,24},{20,28},{24,16},{28,20},{1,9},{5... | collective-permute-start | bytes 1572872 | tf_op jit(solution)/shard_map/ppermute | solution.py:383
  273.2 108.2 %collective-permute-start.52 = (bf16[512,2048]{1,0:T(8,128)(2,1)S(1)}, bf16[512,2048]{1,0:T(8,128)(2,1)S(1)}, u32[]{:S(2)}, u32[]{:S(2)}) collective-permute-start(bf16[512,2048]{1,0:T(8,128)(2,1)S(1)} %copy-done.27), channel_id=1, source_target_pairs={{0,1},{1,0},{2,3},{3,2},{4,5},{5,4},{6,7},{7,6},{8,9},{9,8},{10,11... | collective-permute-start | bytes 6291464 | tf_op jit(solution)/shard_map/ppermute | solution.py:355
  293.3 60.5 %collective-permute-start.47 = (bf16[2,2,2,128,256]{4,3,2,1,0:T(8,128)(2,1)S(1)}, bf16[2,2,2,128,256]{4,3,2,1,0:T(8,128)(2,1)S(1)}, u32[]{:S(2)}, u32[]{:S(2)}) collective-permute-start(bf16[2,2,2,128,256]{4,3,2,1,0:T(8,128)(2,1)S(1)} %constant_dynamic-slice_fusion.7), channel_id=1, source_target_pairs={{0,2},{1,3},{2,0},{3,1},{4,6},{5,7},{6,4},{7,5},{8,10},{9,11},{10,... | collective-permute-start | bytes 1572872 | tf_op jit(solution)/shard_map/ppermute | solution.py:358
  322.9 31.7 %collective-permute-start.33 = (bf16[2,2,1,128,512]{4,3,2,1,0:T(8,128)(2,1)S(1)}, bf16[2,2,1,128,512]{4,3,2,1,0:T(8,128)(2,1)S(1)}, u32[]{:S(2)}, u32[]{:S(2)}) collective-permute-start(bf16[2,2,1,128,512]{4,3,2,1,0:T(8,128)(2,1)S(1)} %constant_dynamic-slice_fusion.2), channel_id=1, source_target_pairs={{0,4},{4,0},{8,12},{12,8},{16,20},{20,16},{24,28},{28,24},{1,5},{5... | collective-permute-start | bytes 1572872 | tf_op jit(solution)/shard_map/ppermute | solution.py:383
  363.3 31.6 %collective-permute-start.9 = (bf16[3,512,512]{2,1,0:T(8,128)(2,1)S(1)}, bf16[3,512,512]{2,1,0:T(8,128)(2,1)S(1)}, u32[]{:S(2)}, u32[]{:S(2)}) collective-permute-start(bf16[3,512,512]{2,1,0:T(8,128)(2,1)S(1)} %pad_maximum_fusion.5), channel_id=1, source_target_pairs={{0,1},{1,0},{2,3},{3,2},{4,5},{5,4},{6,7},{7,6},{8,9},{9,8},{10,11... | collective-permute-start | bytes 4718600 | tf_op jit(solution)/shard_map/ppermute | solution.py:355
  376.2 38.3 %collective-permute-start.36 = (bf16[1,1,1,128,256]{4,3,2,1,0:T(8,128)(2,1)}, bf16[1,1,1,128,256]{4,3,2,1,0:T(8,128)(2,1)}, u32[]{:S(2)}, u32[]{:S(2)}) collective-permute-start(bf16[1,1,1,128,256]{4,3,2,1,0:T(8,128)(2,1)} %add_convert_fusion.29), channel_id=1, source_target_pairs={{0,16},{4,20},{8,24},{12,28},{16,0},{20,4},{24,8},{28,12},{1,17},{... | collective-permute-start | bytes 196616 | tf_op jit(solution)/shard_map/ppermute | solution.py:383
  379.5 37.3 %collective-permute-start.30 = (bf16[1,1,1,128,256]{4,3,2,1,0:T(8,128)(2,1)}, bf16[1,1,1,128,256]{4,3,2,1,0:T(8,128)(2,1)}, u32[]{:S(2)}, u32[]{:S(2)}) collective-permute-start(bf16[1,1,1,128,256]{4,3,2,1,0:T(8,128)(2,1)} %add_convert_fusion.30), channel_id=1, source_target_pairs={{0,16},{4,20},{8,24},{12,28},{16,0},{20,4},{24,8},{28,12},{1,17},{... | collective-permute-start | bytes 196616 | tf_op jit(solution)/shard_map/ppermute | solution.py:383
  391.0 65.4 %collective-permute-start.53 = (bf16[2,1,2,128,2048]{4,3,2,1,0:T(8,128)(2,1)}, bf16[2,1,2,128,2048]{4,3,2,1,0:T(8,128)(2,1)S(1)}, u32[]{:S(2)}, u32[]{:S(2)}) collective-permute-start(bf16[2,1,2,128,2048]{4,3,2,1,0:T(8,128)(2,1)} %constant_dynamic-slice_fusion), channel_id=1, source_target_pairs={{0,8},{4,12},{8,0},{12,4},{16,24},{20,28},{24,16},{28,20},{1,9},{5... | collective-permute-start | bytes 6291464 | tf_op jit(solution)/shard_map/ppermute | solution.py:383
  412.0 46.4 %collective-permute-start.59 = (bf16[2,2,1,512,512]{4,3,2,1,0:T(8,128)(2,1)S(1)}, bf16[2,2,1,512,512]{4,3,2,1,0:T(8,128)(2,1)S(1)}, u32[]{:S(2)}, u32[]{:S(2)}) collective-permute-start(bf16[2,2,1,512,512]{4,3,2,1,0:T(8,128)(2,1)S(1)} %constant_dynamic-slice_fusion.19), channel_id=1, source_target_pairs={{0,4},{4,0},{8,12},{12,8},{16,20},{20,16},{24,28},{28,24},{1,5},{5... | collective-permute-start | bytes 6291464 | tf_op jit(solution)/shard_map/ppermute | solution.py:383
  420.1 35.1 %collective-permute-start.65 = (f32[2,1024]{1,0:T(2,128)S(1)}, f32[2,1024]{1,0:T(2,128)S(1)}, u32[]{:S(2)}, u32[]{:S(2)}) collective-permute-start(f32[2,1024]{1,0:T(2,128)S(1)} %fusion.317), channel_id=1, source_target_pairs={{0,4},{4,0},{8,12},{12,8},{16,20},{20,16},{24,28},{28,24},{1,5},{5... | collective-permute-start | bytes 24584 | tf_op jit(solution)/shard_map/ppermute | solution.py:383
  456.8 44.3 %collective-permute-start.54 = (bf16[1,1,2,128,2048]{4,3,2,1,0:T(8,128)(2,1)S(1)}, bf16[1,1,2,128,2048]{4,3,2,1,0:T(8,128)(2,1)S(1)}, u32[]{:S(2)}, u32[]{:S(2)}) collective-permute-start(bf16[1,1,2,128,2048]{4,3,2,1,0:T(8,128)(2,1)S(1)} %add_convert_fusion.2), channel_id=1, source_target_pairs={{0,16},{4,20},{8,24},{12,28},{16,0},{20,4},{24,8},{28,12},{1,17},{... | collective-permute-start | bytes 3145736 | tf_op jit(solution)/shard_map/ppermute | solution.py:383
  459.0 44.2 %collective-permute-start.60 = (bf16[2,2,1,512,256]{4,3,2,1,0:T(8,128)(2,1)S(1)}, bf16[2,2,1,512,256]{4,3,2,1,0:T(8,128)(2,1)S(1)}, u32[]{:S(2)}, u32[]{:S(2)}) collective-permute-start(bf16[2,2,1,512,256]{4,3,2,1,0:T(8,128)(2,1)S(1)} %add_convert_fusion.1), channel_id=1, source_target_pairs={{0,2},{1,3},{2,0},{3,1},{4,6},{5,7},{6,4},{7,5},{8,10},{9,11},{10,... | collective-permute-start | bytes 3145736 | tf_op jit(solution)/shard_map/ppermute | solution.py:358
  459.6 40.9 %collective-permute-start.67 = (f32[2,1024]{1,0:T(2,128)S(1)}, f32[2,1024]{1,0:T(2,128)S(1)}, u32[]{:S(2)}, u32[]{:S(2)}) collective-permute-start(f32[2,1024]{1,0:T(2,128)S(1)} %add.1616), channel_id=1, source_target_pairs={{0,16},{4,20},{8,24},{12,28},{16,0},{20,4},{24,8},{28,12},{1,17},{... | collective-permute-start | bytes 24584 | tf_op jit(solution)/shard_map/ppermute | solution.py:383
  461.9 42.7 %collective-permute-start.10 = (bf16[256,1024]{1,0:T(8,128)(2,1)S(1)}, bf16[256,1024]{1,0:T(8,128)(2,1)S(1)}, u32[]{:S(2)}, u32[]{:S(2)}) collective-permute-start(bf16[256,1024]{1,0:T(8,128)(2,1)S(1)} %slice.598), channel_id=1, source_target_pairs={{0,2},{1,3},{2,0},{3,1},{4,6},{5,7},{6,4},{7,5},{8,10},{9,11},{10,... | collective-permute-start | bytes 1572872 | tf_op jit(solution)/shard_map/ppermute | solution.py:358
  (173 other events, 1599.8 us)
